TPU v7x, 512 devices: a whole 4x4x16 slice. The times are simulated.
512 devices in a mesh: param: 16 (over y, x), dom: 32 (over z, core).
Axes of the slice: x: 4, y: 4, z: 16, core: 2. Of those that a mesh axis runs over, the one named last changes fastest.
Arguments:
- particles: bfloat16 [512, 524288], P('dom', 'param'), may hold values from -40 to 40
- scores: bfloat16 [512, 524288], P('dom', 'param'), may hold values from -6 to 6
- basis: bfloat16 [524288, 128], P(('param', 'dom')), may hold values from -0.0078125 to 0.0078125
Outputs:
- velocity: bfloat16 [512, 524288], P('dom', 'param')
- phi: float32 [512, 128], P('dom')
All inputs are finite; a program needn't handle non-finite values.
Results may differ from a plain program's by a relative error of at most 0.0049.
Values may be sent and summed in bfloat16 or wider, within the bound.
No kernel may reach another device: no remote copies, remote signals or barrier semaphores. Data moves between devices by JAX's collectives and lax.ppermute only.
A program may use at most 64 MiB of HBM per device.

v0:
```python
import math
import jax
import jax.numpy as jnp
from jax import lax
from jax.sharding import Mesh, PartitionSpec as P

P_SIZE = 524288
R = 128
TAIL = 16
TOP = 15.0


def swap_cores(array):
    return lax.ppermute(array, "core", [(0, 1), (1, 0)])


def packed_shard(basis):
    wide = basis.astype(jnp.float32)
    largest = jnp.maximum(jnp.max(jnp.abs(wide)), 1e-30)
    power = jnp.ceil(jnp.log2(largest))
    scaled = (wide * jnp.exp2(TOP - power)).astype(jnp.float16)
    tail = jnp.full((TAIL, basis.shape[1]), power, jnp.float32).astype(jnp.float16)
    return jnp.concatenate([scaled, tail], axis=0)


def unpacked(gathered, shards):
    rows = gathered.reshape(shards, -1, gathered.shape[1])
    power = rows[:, -TAIL:, :].astype(jnp.float32)[:, :1, :1]
    wide = rows[:, :-TAIL, :].astype(jnp.float32) * jnp.exp2(power - TOP)
    return wide.astype(jnp.bfloat16)


def stein_terms(own, every, every_score):
    count = every.shape[0]
    every_sq = jnp.sum(every * every, axis=1)
    own_sq = jnp.sum(own * own, axis=1)
    center = jnp.mean(every, axis=0)
    width = 2.0 * (jnp.mean(every_sq) - jnp.sum(center * center)) / math.log(count) + 1e-06
    cross = jnp.dot(own, every.T, precision=lax.Precision.HIGHEST)
    dist = own_sq[:, None] + every_sq[None, :] - 2.0 * cross
    kern = jnp.exp(-dist / width)
    drive = jnp.dot(kern, every_score, precision=lax.Precision.HIGHEST)
    pull = jnp.dot(kern, every, precision=lax.Precision.HIGHEST)
    total = jnp.sum(kern, axis=1)
    return (drive + 2.0 / width * (own * total[:, None] - pull)) / count


def sent_to_all(array, axis):
    peers = lax.axis_size(axis)
    return lax.all_to_all(
        jnp.broadcast_to(array[None], (peers, *array.shape)), axis, 0, 0, tiled=True
    )


def contract(rows, half_basis):
    return lax.dot_general(
        rows, half_basis, (((1, 2), (0, 1)), ((), ())), preferred_element_type=jnp.float32
    )


def lift(phi_low, half_basis):
    lifted = lax.dot_general(
        phi_low, half_basis, (((1,), (2,)), ((), ())), preferred_element_type=jnp.float32
    )
    return (lifted * math.sqrt(P_SIZE / R)).astype(jnp.bfloat16)


def body(particles, scores, basis):
    rows = particles.shape[0]
    depth = basis.shape[0]
    shards = lax.axis_size("z")
    core = lax.axis_index("core")
    both = jnp.concatenate([particles, scores], axis=0).reshape(2 * rows, shards, 2, depth)
    theirs = lax.dynamic_index_in_dim(both, 1 - core, 2, keepdims=False)
    mine = lax.dynamic_index_in_dim(both, core, 2, keepdims=False)
    others = swap_cores(theirs)
    gathered = lax.all_gather(packed_shard(basis), "z", axis=0, tiled=True)
    half = unpacked(gathered, shards)
    other_half = swap_cores(half)
    own_part = contract(mine, half)
    other_part = contract(others, half)
    own_part = jnp.concatenate([own_part[:rows], own_part[rows:]], axis=1)
    other_part = jnp.concatenate([other_part[:rows], other_part[rows:]], axis=1)
    first = jnp.where(core == 0, own_part, other_part)
    second = jnp.where(core == 0, other_part, own_part)
    pair = jnp.stack([first, second])
    peers = lax.axis_size("param")
    pieces = jnp.broadcast_to(pair[None], (peers, *pair.shape)).reshape(2 * peers, rows, -1)
    summed = lax.all_to_all(pieces, ("param", "core"), 0, 0, tiled=True).sum(axis=0)
    column = sent_to_all(summed, "z").reshape(shards * rows, -1)
    everyone = lax.all_gather(column, "core", axis=0, tiled=True)
    phi = stein_terms(summed[:, :R], everyone[:, :R], everyone[:, R:])
    phi_low = phi.astype(jnp.bfloat16)
    ours = lift(phi_low, half)
    rest = lift(phi_low, other_half)
    low = jnp.where(core == 0, ours, rest)
    high = jnp.where(core == 0, rest, ours)
    velocity = jnp.stack([low, high], axis=2).reshape(particles.shape)
    return (velocity, phi)


def solution(mesh):
    inner = Mesh(mesh.devices.reshape(mesh.devices.shape[0], -1, 2), ("param", "z", "core"))
    dom = ("z", "core")
    in_specs = (P(dom, "param"), P(dom, "param"), P(("param", "z", "core"), None))
    out_specs = (P(dom, "param"), P(dom, None))
    return jax.shard_map(body, mesh=inner, in_specs=in_specs, out_specs=out_specs, check_vma=False)
```

profile of v0, /device:TPU:1, one launch (start us, length us, event | category | flops | bytes accessed | tf_op | source)
XLA Modules:
  0.0 163.5 jit_solution(3833632551950099239)
XLA Ops:
  0.6 3.0 %pad_maximum_fusion = bf16[32,32768]{1,0:T(8,128)(2,1)} fusion(bf16[16,32768]{1,0:T(8,128)(2,1)} %param.4, bf16[16,32768]{1,0:T(8,128)(2,1)} %param.3), kind=kLoop, calls=%fused_computation.1 | loop fusion | flops 4194304 | bytes 4194304 | tf_op jit(solution)/shard_map/concatenate | solution.py:73
  3.7 3.3 %reshape.134 = bf16[32,16,2,1024]{3,2,1,0:T(2,128)(2,1)S(1)} reshape(bf16[32,32768]{1,0:T(8,128)(2,1)} %pad_maximum_fusion) | data formatting | bytes 4194304 | tf_op jit(solution)/shard_map/reshape | solution.py:73
  7.0 5.8 %constant_dynamic-slice_fusion.1 = (bf16[32,16,1,1024]{3,2,1,0:T(2,128)(2,1)}, bf16[32,16,1,1024]{3,2,1,0:T(2,128)(2,1)S(1)}) fusion(bf16[32,16,2,1024]{3,2,1,0:T(2,128)(2,1)S(1)} %reshape.134, s32[]{:T(128)S(6)} %select_n.47, s32[]{:T(128)S(6)} %select_n.48), kind=kLoop, calls=%fused_computation.51 | loop fusion | bytes 4194312 | tf_op jit(solution)/shard_map/jit(dynamic_index_in_dim)/dynamic_slice | solution.py:75
  12.7 1.1 copy.30
  13.9 8.8 %collective-permute-start = (bf16[32,16,1024]{2,0,1:T(8,128)(2,1)S(1)}, bf16[32,16,1024]{2,0,1:T(8,128)(2,1)}, u32[]{:S(2)}, u32[]{:S(2)}) collective-permute-start(bf16[32,16,1024]{2,0,1:T(8,128)(2,1)S(1)} %bitcast.44), channel_id=1, source_target_pairs={{0,1},{1,0},{2,3},{3,2},{4,5},{5,4},{6,7},{7,6},{8,9},{9,8},{10,11... | collective-permute-start | bytes 3145736 | tf_op jit(solution)/shard_map/ppermute | solution.py:14
  22.7 0.6 fusion.9
  24.1 0.1 fusion.10
  24.1 0.1 concatenate.49
  24.2 56.2 %all-gather.1 = f16[16640,128]{1,0:T(8,128)(2,1)S(1)} all-gather(f16[1040,128]{1,0:T(8,128)(2,1)S(1)} %concatenate.49), channel_id=1, replica_groups=mesh['param'=16,'z'=16,'core'=2] {'z'}, dimensions={0}, use_global_device_ids=true | all-gather | bytes 4526080 | tf_op jit(solution)/shard_map/all_gather | solution.py:77
  80.4 2.0 %copy-done = f16[16640,128]{1,0:T(8,128)(2,1)} copy-done((f16[16640,128]{1,0:T(8,128)(2,1)}, f16[16640,128]{1,0:T(8,128)(2,1)S(1)}, u32[]{:S(2)}) %copy-start) | copy-done | bytes 4259864
  82.3 0.1 copy.25
  82.4 5.4 %multiply_convert_fusion = bf16[16,1024,128]{2,1,0:T(8,128)(2,1)} fusion(f16[16,1040,128]{2,1,0:T(8,128)(2,1)} %bitcast.42, f32[16]{0:T(128)S(1)} %exponential_bitcast_fusion), kind=kLoop, calls=%fused_computation | loop fusion | flops 6291456 | bytes 8388672 | tf_op jit(solution)/shard_map/convert_element_type | solution.py:30
  87.9 7.8 %collective-permute-start.1 = (bf16[16,1024,128]{2,1,0:T(8,128)(2,1)}, bf16[16,1024,128]{2,1,0:T(8,128)(2,1)}, u32[]{:S(2)}, u32[]{:S(2)}) collective-permute-start(bf16[16,1024,128]{2,1,0:T(8,128)(2,1)} %multiply_convert_fusion), channel_id=1, source_target_pairs={{0,1},{1,0},{2,3},{3,2},{4,5},{5,4},{6,7},{7,6},{8,9},{9,8},{10,11... | collective-permute-start | bytes 12582920 | tf_op jit(solution)/shard_map/ppermute | solution.py:14
  95.7 3.6 %convolution_bitcast_fusion.1 = f32[32,128]{1,0:T(8,128)S(1)} fusion(bf16[16,1024,128]{2,1,0:T(8,128)(2,1)} %multiply_convert_fusion, bf16[32,16,1,1024]{3,2,1,0:T(2,128)(2,1)S(1)} %copy-done.1), kind=kOutput, calls=%fused_computation.12 | convolution fusion | flops 134217728 | bytes 5259264 | tf_op jit(solution)/shard_map/dot_general | solution.py:56
  99.3 3.3 %convolution_bitcast_fusion = f32[32,128]{1,0:T(8,128)S(1)} fusion(bf16[32,16,1024]{2,0,1:T(8,128)(2,1)} %collective-permute-done, bf16[16,1024,128]{2,1,0:T(8,128)(2,1)} %multiply_convert_fusion), kind=kOutput, calls=%fused_computation.11 | convolution fusion | flops 134217728 | bytes 5259264 | tf_op jit(solution)/shard_map/dot_general | solution.py:56
  102.6 0.1 broadcast_in_dim.4
  102.7 18.5 %all_to_all.10 = f32[32,16,256]{2,1,0:T(8,128)S(1)} all-to-all(f32[32,16,256]{2,1,0:T(8,128)S(1)} %bitcast.43), channel_id=1, replica_groups=mesh['param'=16,'z'=16,'core'=2] {'param','core'}, dimensions={0} | all-to-all | bytes 1048576 | tf_op jit(solution)/shard_map/all_to_all | solution.py:89
  121.3 0.7 broadcast_in_dim.5
  122.0 7.2 %all-to-all-start.1 = ((f32[16,16,256]{2,1,0:T(8,128)}), f32[16,16,256]{2,1,0:T(8,128)S(1)}, u32[]{:S(2)}, u32[]{:S(2)}) async-start(f32[16,16,256]{2,1,0:T(8,128)} %broadcast_in_dim.5), calls=%async_computation.1 | async-start | bytes 524288 | tf_op jit(solution)/shard_map/all_to_all | solution.py:50
  129.2 0.1 multiply_reduce_fusion.2
  129.3 13.7 %all-to-all-done.1 = f32[16,16,256]{2,1,0:T(8,128)S(1)} async-done(((f32[16,16,256]{2,1,0:T(8,128)}), f32[16,16,256]{2,1,0:T(8,128)S(1)}, u32[]{:S(2)}, u32[]{:S(2)}) %all-to-all-start.1) | async-done | bytes 262176 | tf_op jit(solution)/shard_map/all_to_all | solution.py:50
  143.0 7.3 %all_gather.7 = f32[512,256]{1,0:T(8,128)S(1)} all-gather(f32[256,256]{1,0:T(8,128)S(1)} %bitcast.45), channel_id=1, replica_groups=mesh['param'=16,'z'=16,'core'=2] {'core'}, dimensions={0}, use_global_device_ids=true | all-gather | bytes 786432 | tf_op jit(solution)/shard_map/all_gather | solution.py:91
  150.3 0.7 multiply_reduce_fusion.1
  151.7 0.6 multiply_reduce_fusion.3
  152.9 0.4 fusion.22
  153.4 0.2 fusion.11
  153.6 0.3 fusion.8
  153.9 3.4 %fusion = bf16[16,16,1024]{2,0,1:T(8,128)(2,1)S(1)} fusion(bf16[16,1024,128]{2,1,0:T(8,128)(2,1)} %multiply_convert_fusion, f32[16,128]{1,0:T(8,128)S(1)} %fusion.8), kind=kOutput, calls=%fused_computation.4 | convolution fusion | flops 67635200 | bytes 4726784 | tf_op jit(solution)/shard_map/dot_general | solution.py:62
  157.3 3.4 %select_bitcast_fusion.1 = (bf16[16,16,1,1024]{3,0,1,2:T(8,128)(2,1)S(1)}, bf16[16,16,1,1024]{3,0,1,2:T(8,128)(2,1)S(1)}) fusion(bf16[16,16,1024]{2,0,1:T(8,128)(2,1)S(1)} %fusion, pred[]{:T(512)S(6)} %eq.2, bf16[16,1024,128]{2,1,0:T(8,128)(2,1)} %collective-permute-done.1, f32[16,128]{1,0:T(8,128)S(1)} %fusion.8), kind=kOutput, calls=%fused_computation.25 | convolution fusion | flops 68159488 | bytes 5775361 | tf_op jit(solution)/shard_map/dot_general | solution.py:62
  160.7 0.1 pad_maximum_fusion.1
  160.8 1.1 copy.23
  161.9 1.6 reshape.138
  (16 shorter events, 0.1 us)
Async XLA Ops:
  7.0 15.7 %copy-start.2 = (bf16[1024,128]{1,0:T(8,128)(2,1)S(1)}, bf16[1024,128]{1,0:T(8,128)(2,1)}, u32[]{:S(2)}) copy-start(bf16[1024,128]{1,0:T(8,128)(2,1)} %param.5) | copy-start | bytes 786436
  13.9 85.4 %collective-permute-start = (bf16[32,16,1024]{2,0,1:T(8,128)(2,1)S(1)}, bf16[32,16,1024]{2,0,1:T(8,128)(2,1)}, u32[]{:S(2)}, u32[]{:S(2)}) collective-permute-start(bf16[32,16,1024]{2,0,1:T(8,128)(2,1)S(1)} %bitcast.44), channel_id=1, source_target_pairs={{0,1},{1,0},{2,3},{3,2},{4,5},{5,4},{6,7},{7,6},{8,9},{9,8},{10,11... | collective-permute-start | bytes 3145736 | tf_op jit(solution)/shard_map/ppermute | solution.py:14
  80.4 2.0 %copy-start = (f16[16640,128]{1,0:T(8,128)(2,1)}, f16[16640,128]{1,0:T(8,128)(2,1)S(1)}, u32[]{:S(2)}) copy-start(f16[16640,128]{1,0:T(8,128)(2,1)S(1)} %all-gather.1) | copy-start | bytes 12779524
  82.4 13.2 %copy-start.1 = (bf16[32,16,1,1024]{3,2,1,0:T(2,128)(2,1)S(1)}, bf16[32,16,1,1024]{3,2,1,0:T(2,128)(2,1)}, u32[]{:S(2)}) copy-start(bf16[32,16,1,1024]{3,2,1,0:T(2,128)(2,1)} %get-tuple-element.5) | copy-start | bytes 3145732
  87.9 69.4 %collective-permute-start.1 = (bf16[16,1024,128]{2,1,0:T(8,128)(2,1)}, bf16[16,1024,128]{2,1,0:T(8,128)(2,1)}, u32[]{:S(2)}, u32[]{:S(2)}) collective-permute-start(bf16[16,1024,128]{2,1,0:T(8,128)(2,1)} %multiply_convert_fusion), channel_id=1, source_target_pairs={{0,1},{1,0},{2,3},{3,2},{4,5},{5,4},{6,7},{7,6},{8,9},{9,8},{10,11... | collective-permute-start | bytes 12582920 | tf_op jit(solution)/shard_map/ppermute | solution.py:14
  122.0 21.0 %all-to-all-start.1 = ((f32[16,16,256]{2,1,0:T(8,128)}), f32[16,16,256]{2,1,0:T(8,128)S(1)}, u32[]{:S(2)}, u32[]{:S(2)}) async-start(f32[16,16,256]{2,1,0:T(8,128)} %broadcast_in_dim.5), calls=%async_computation.1 | async-start | bytes 524288 | tf_op jit(solution)/shard_map/all_to_all | solution.py:50
  153.9 6.8 %copy-start.3 = (f32[16,128]{1,0:T(8,128)}, f32[16,128]{1,0:T(8,128)S(1)}, u32[]{:S(2)}) copy-start(f32[16,128]{1,0:T(8,128)S(1)} %fusion.8) | copy-start | bytes 24580
where the time goes:
time: 164 us
  blocking collectives  82 us (50%)
  starting transfers between devices  23.7 us (14%)
  local copies, waits for them, and re-layouts  15.8 us (10%)
  matrix products  14.6 us (9%)
  waiting for transfers between devices  13.7 us (8%)
  other arithmetic  10.8 us (7%)
  between operations  2.92 us (2%)
    all_gather x1, blocking collectives, body(): gathered = lax.all_gather(packed_shard(basis), 'z', axis=0, tiled=True)  56.2 us
    all_to_all x1, blocking collectives, body(): lax.all_to_all(pieces, ('param', 'core'), 0, 0, tiled=True).sum(axis=0)  18.5 us
    ppermute x2, starting transfers between devices, swap_cores(): return lax.ppermute(array, 'core', [(0, 1), (1, 0)])  16.6 us
    all_to_all x1, waiting for transfers between devices, sent_to_all(): lax.all_to_all(jnp.broadcast_to(array[None], (peers, *array.shape)), axis...  13.7 us
    all_gather x1, blocking collectives, body(): everyone = lax.all_gather(column, 'core', axis=0, tiled=True)  7.34 us
    all_to_all x1, starting transfers between devices, sent_to_all(): lax.all_to_all(jnp.broadcast_to(array[None], (peers, *array.shape)), axis...  7.17 us
    dot_general x2, matrix products, contract(): lax.dot_general(rows, half_basis, (((1, 2), (0, 1)), ((), ())), preferred...  6.84 us
    dot_general x2, matrix products, lift(): lax.dot_general(phi_low, half_basis, (((1,), (2,)), ((), ())), preferred_...  6.78 us
  transfers between devices with their start and end apart: 3, of which 1 were waited for; matrix products, arithmetic and copies ran while one was open for 12% of the time, Pallas kernels for 0%

commit v1 on v0

--- a/solution.py
+++ b/solution.py
@@ -74,7 +74,9 @@
     theirs = lax.dynamic_index_in_dim(both, 1 - core, 2, keepdims=False)
     mine = lax.dynamic_index_in_dim(both, core, 2, keepdims=False)
     others = swap_cores(theirs)
-    gathered = lax.all_gather(packed_shard(basis), "z", axis=0, tiled=True)
+    gathered = jnp.concatenate(
+        lax.all_to_all(jnp.stack([packed_shard(basis)] * lax.axis_size("z")), "z", 0, 0), axis=0
+    )
     half = unpacked(gathered, shards)
     other_half = swap_cores(half)
     own_part = contract(mine, half)

time: 164 us -> 288 us (1.76)
  waiting for transfers between devices: 13.7 us -> 184 us
  blocking collectives: 82 us -> 25.9 us
  starting transfers between devices: 23.7 us -> 32.5 us
    all_to_all x0 -> x1, waiting for transfers between devices: none -> 170 us  [body(): lax.all_to_all(jnp.stack([packed_shard(basis)] * lax.axis_size('z')), 'z'...]
    all_gather x1 -> x0, blocking collectives: 56.2 us -> none  [body(): gathered = lax.all_gather(packed_shard(basis), 'z', axis=0, tiled=True)]
    all_to_all x0 -> x1, starting transfers between devices: none -> 15.9 us  [body(): lax.all_to_all(jnp.stack([packed_shard(basis)] * lax.axis_size('z')), 'z'...]
    ppermute x2, starting transfers between devices: 16.6 us -> 6.35 us  [swap_cores(): return lax.ppermute(array, 'core', [(0, 1), (1, 0)])]
    all_to_all x1, starting transfers between devices: 7.17 us -> 10.2 us  [sent_to_all(): lax.all_to_all(jnp.broadcast_to(array[None], (peers, *array.shape)), axis...]
  transfers between devices with their start and end apart: 3 -> 4, of which waited for: 1 -> 2; matrix products, arithmetic and copies ran while one was open for 12% -> 11% of each run, Pallas kernels for 0% -> 0%
where the time goes in v1:
time: 288 us; the launch traced here: 287 us
  waiting for transfers between devices  184 us (64%)
  starting transfers between devices  32.5 us (11%)
  blocking collectives  25.9 us (9%)
  local copies, waits for them, and re-layouts  17.2 us (6%)
  matrix products  14.3 us (5%)
  other arithmetic  11 us (4%)
  between operations  2.92 us (1%)
    all_to_all x1, waiting for transfers between devices, body(): lax.all_to_all(jnp.stack([packed_shard(basis)] * lax.axis_size('z')), 'z'...  170 us
    all_to_all x1, blocking collectives, body(): lax.all_to_all(pieces, ('param', 'core'), 0, 0, tiled=True).sum(axis=0)  18.5 us
    all_to_all x1, starting transfers between devices, body(): lax.all_to_all(jnp.stack([packed_shard(basis)] * lax.axis_size('z')), 'z'...  15.9 us
    all_to_all x1, waiting for transfers between devices, sent_to_all(): lax.all_to_all(jnp.broadcast_to(array[None], (peers, *array.shape)), axis...  13.7 us
    all_to_all x1, starting transfers between devices, sent_to_all(): lax.all_to_all(jnp.broadcast_to(array[None], (peers, *array.shape)), axis...  10.2 us
    all_gather x1, blocking collectives, body(): everyone = lax.all_gather(column, 'core', axis=0, tiled=True)  7.34 us
    dot_general x2, matrix products, lift(): lax.dot_general(phi_low, half_basis, (((1,), (2,)), ((), ())), preferred_...  6.78 us
    dot_general x2, matrix products, contract(): lax.dot_general(rows, half_basis, (((1, 2), (0, 1)), ((), ())), preferred...  6.62 us
  transfers between devices with their start and end apart: 4, of which 2 were waited for; matrix products, arithmetic and copies ran while one was open for 11% of the time, Pallas kernels for 0%

profile of v1, /device:TPU:1, one launch (start us, length us, event | category | flops | bytes accessed | tf_op | source)
XLA Modules:
  0.0 287.5 jit_solution(1026330558617370441)
XLA Ops:
  0.6 1.6 fusion.9
  3.0 1.0 fusion.10
  4.1 2.6 stack.10
  6.6 15.9 %all-to-all-start = ((f16[16,1040,128]{2,1,0:T(8,128)(2,1)}), f16[16,1040,128]{2,1,0:T(8,128)(2,1)}, u32[]{:S(2)}, u32[]{:S(2)}) async-start(f16[16,1040,128]{2,1,0:T(8,128)(2,1)} %stack.10), calls=%async_computation | async-start | bytes 8519680 | tf_op jit(solution)/shard_map/all_to_all | solution.py:78
  22.6 1.5 pad_maximum_fusion
  24.1 3.3 %reshape.133 = bf16[32,16,2,1024]{3,2,1,0:T(2,128)(2,1)S(1)} reshape(bf16[32,32768]{1,0:T(8,128)(2,1)} %pad_maximum_fusion) | data formatting | bytes 4194304 | tf_op jit(solution)/shard_map/reshape | solution.py:73
  27.4 5.8 %constant_dynamic-slice_fusion.1 = (bf16[32,16,1,1024]{3,2,1,0:T(2,128)(2,1)}, bf16[32,16,1,1024]{3,2,1,0:T(2,128)(2,1)S(1)}) fusion(bf16[32,16,2,1024]{3,2,1,0:T(2,128)(2,1)S(1)} %reshape.133, s32[]{:T(128)S(6)} %select_n.47, s32[]{:T(128)S(6)} %select_n.48), kind=kLoop, calls=%fused_computation.51 | loop fusion | bytes 4194312 | tf_op jit(solution)/shard_map/jit(dynamic_index_in_dim)/dynamic_slice | solution.py:75
  33.1 1.1 copy.30
  34.3 2.9 collective-permute-start
  37.1 170.0 %all-to-all-done = f16[16,1040,128]{2,1,0:T(8,128)(2,1)} async-done(((f16[16,1040,128]{2,1,0:T(8,128)(2,1)}), f16[16,1040,128]{2,1,0:T(8,128)(2,1)}, u32[]{:S(2)}, u32[]{:S(2)}) %all-to-all-start) | async-done | bytes 4259872 | tf_op jit(solution)/shard_map/all_to_all | solution.py:78
  207.2 0.8 slice.43
  207.9 0.1 copy.25
  208.0 5.3 %multiply_convert_fusion = bf16[16,1024,128]{2,1,0:T(8,128)(2,1)} fusion(f16[16,1040,128]{2,1,0:T(8,128)(2,1)} %all-to-all-done, f32[16]{0:T(128)S(1)} %exponential_bitcast_fusion), kind=kLoop, calls=%fused_computation | loop fusion | flops 6291456 | bytes 8388672 | tf_op jit(solution)/shard_map/convert_element_type | solution.py:30
  213.3 3.5 %collective-permute-start.1 = (bf16[16,1024,128]{2,1,0:T(8,128)(2,1)}, bf16[16,1024,128]{2,1,0:T(8,128)(2,1)}, u32[]{:S(2)}, u32[]{:S(2)}) collective-permute-start(bf16[16,1024,128]{2,1,0:T(8,128)(2,1)} %multiply_convert_fusion), channel_id=1, source_target_pairs={{0,1},{1,0},{2,3},{3,2},{4,5},{5,4},{6,7},{7,6},{8,9},{9,8},{10,11... | collective-permute-start | bytes 12582920 | tf_op jit(solution)/shard_map/ppermute | solution.py:14
  216.8 2.9 %convolution_bitcast_fusion = f32[32,128]{1,0:T(8,128)S(1)} fusion(bf16[32,16,1024]{2,0,1:T(8,128)(2,1)S(1)} %collective-permute-done, bf16[16,1024,128]{2,1,0:T(8,128)(2,1)} %multiply_convert_fusion), kind=kOutput, calls=%fused_computation.11 | convolution fusion | flops 134217728 | bytes 5259264 | tf_op jit(solution)/shard_map/dot_general | solution.py:56
  219.8 3.7 %convolution_bitcast_fusion.1 = f32[32,128]{1,0:T(8,128)S(1)} fusion(bf16[16,1024,128]{2,1,0:T(8,128)(2,1)} %multiply_convert_fusion, bf16[32,16,1,1024]{3,2,1,0:T(2,128)(2,1)S(1)} %copy-done), kind=kOutput, calls=%fused_computation.12 | convolution fusion | flops 134217728 | bytes 5259264 | tf_op jit(solution)/shard_map/dot_general | solution.py:56
  223.6 18.5 %all_to_all.15 = f32[32,16,256]{2,1,0:T(8,128)S(1)} all-to-all(f32[32,16,256]{2,1,0:T(8,128)S(1)} %bitcast.40), channel_id=1, replica_groups=mesh['param'=16,'z'=16,'core'=2] {'param','core'}, dimensions={0} | all-to-all | bytes 1048576 | tf_op jit(solution)/shard_map/all_to_all | solution.py:91
  242.2 0.7 broadcast_in_dim.5
  242.9 10.2 %all-to-all-start.2 = ((f32[16,16,256]{2,1,0:T(8,128)}), f32[16,16,256]{2,1,0:T(8,128)S(1)}, u32[]{:S(2)}, u32[]{:S(2)}) async-start(f32[16,16,256]{2,1,0:T(8,128)} %broadcast_in_dim.5), calls=%async_computation.2 | async-start | bytes 524288 | tf_op jit(solution)/shard_map/all_to_all | solution.py:50
  253.1 0.1 multiply_reduce_fusion.2
  253.2 13.7 %all-to-all-done.2 = f32[16,16,256]{2,1,0:T(8,128)S(1)} async-done(((f32[16,16,256]{2,1,0:T(8,128)}), f32[16,16,256]{2,1,0:T(8,128)S(1)}, u32[]{:S(2)}, u32[]{:S(2)}) %all-to-all-start.2) | async-done | bytes 262176 | tf_op jit(solution)/shard_map/all_to_all | solution.py:50
  266.9 7.3 %all_gather.3 = f32[512,256]{1,0:T(8,128)S(1)} all-gather(f32[256,256]{1,0:T(8,128)S(1)} %bitcast.42), channel_id=1, replica_groups=mesh['param'=16,'z'=16,'core'=2] {'core'}, dimensions={0}, use_global_device_ids=true | all-gather | bytes 786432 | tf_op jit(solution)/shard_map/all_gather | solution.py:93
  274.3 0.7 multiply_reduce_fusion.1
  275.6 0.6 multiply_reduce_fusion.3
  276.9 0.4 fusion.22
  277.4 0.2 fusion.11
  277.6 0.3 fusion.8
  277.9 3.4 %fusion = bf16[16,16,1024]{2,0,1:T(8,128)(2,1)S(1)} fusion(bf16[16,1024,128]{2,1,0:T(8,128)(2,1)} %multiply_convert_fusion, f32[16,128]{1,0:T(8,128)S(1)} %fusion.8), kind=kOutput, calls=%fused_computation.4 | convolution fusion | flops 67635200 | bytes 4726784 | tf_op jit(solution)/shard_map/dot_general | solution.py:62
  281.3 3.4 %select_bitcast_fusion.1 = (bf16[16,16,1,1024]{3,0,1,2:T(8,128)(2,1)S(1)}, bf16[16,16,1,1024]{3,0,1,2:T(8,128)(2,1)S(1)}) fusion(bf16[16,16,1024]{2,0,1:T(8,128)(2,1)S(1)} %fusion, pred[]{:T(512)S(6)} %eq.2, bf16[16,1024,128]{2,1,0:T(8,128)(2,1)} %collective-permute-done.1, f32[16,128]{1,0:T(8,128)S(1)} %fusion.8), kind=kOutput, calls=%fused_computation.25 | convolution fusion | flops 68159488 | bytes 5775361 | tf_op jit(solution)/shard_map/dot_general | solution.py:62
  284.7 0.1 pad_maximum_fusion.1
  284.8 1.1 copy.23
  285.9 1.6 reshape.136
  (18 shorter events, 0.2 us)
Async XLA Ops:
  6.6 15.9 %copy-start.1 = (bf16[16,32768]{1,0:T(8,128)(2,1)S(1)}, bf16[16,32768]{1,0:T(8,128)(2,1)}, u32[]{:S(2)}) copy-start(bf16[16,32768]{1,0:T(8,128)(2,1)} %param.4) | copy-start | bytes 3145732
  6.6 15.9 %copy-start.2 = (bf16[16,32768]{1,0:T(8,128)(2,1)S(1)}, bf16[16,32768]{1,0:T(8,128)(2,1)}, u32[]{:S(2)}) copy-start(bf16[16,32768]{1,0:T(8,128)(2,1)} %param.3) | copy-start | bytes 3145732
  6.6 200.5 %all-to-all-start = ((f16[16,1040,128]{2,1,0:T(8,128)(2,1)}), f16[16,1040,128]{2,1,0:T(8,128)(2,1)}, u32[]{:S(2)}, u32[]{:S(2)}) async-start(f16[16,1040,128]{2,1,0:T(8,128)(2,1)} %stack.10), calls=%async_computation | async-start | bytes 8519680 | tf_op jit(solution)/shard_map/all_to_all | solution.py:78
  34.3 182.6 %collective-permute-start = (bf16[32,16,1024]{2,0,1:T(8,128)(2,1)S(1)}, bf16[32,16,1024]{2,0,1:T(8,128)(2,1)S(1)}, u32[]{:S(2)}, u32[]{:S(2)}) collective-permute-start(bf16[32,16,1024]{2,0,1:T(8,128)(2,1)S(1)} %bitcast.41), channel_id=1, source_target_pairs={{0,1},{1,0},{2,3},{3,2},{4,5},{5,4},{6,7},{7,6},{8,9},{9,8},{10,11... | collective-permute-start | bytes 3145736 | tf_op jit(solution)/shard_map/ppermute | solution.py:14
  213.3 6.5 %copy-start = (bf16[32,16,1,1024]{3,2,1,0:T(2,128)(2,1)S(1)}, bf16[32,16,1,1024]{3,2,1,0:T(2,128)(2,1)}, u32[]{:S(2)}) copy-start(bf16[32,16,1,1024]{3,2,1,0:T(2,128)(2,1)} %get-tuple-element.5) | copy-start | bytes 3145732
  213.3 67.9 %collective-permute-start.1 = (bf16[16,1024,128]{2,1,0:T(8,128)(2,1)}, bf16[16,1024,128]{2,1,0:T(8,128)(2,1)}, u32[]{:S(2)}, u32[]{:S(2)}) collective-permute-start(bf16[16,1024,128]{2,1,0:T(8,128)(2,1)} %multiply_convert_fusion), channel_id=1, source_target_pairs={{0,1},{1,0},{2,3},{3,2},{4,5},{5,4},{6,7},{7,6},{8,9},{9,8},{10,11... | collective-permute-start | bytes 12582920 | tf_op jit(solution)/shard_map/ppermute | solution.py:14
  242.9 24.0 %all-to-all-start.2 = ((f32[16,16,256]{2,1,0:T(8,128)}), f32[16,16,256]{2,1,0:T(8,128)S(1)}, u32[]{:S(2)}, u32[]{:S(2)}) async-start(f32[16,16,256]{2,1,0:T(8,128)} %broadcast_in_dim.5), calls=%async_computation.2 | async-start | bytes 524288 | tf_op jit(solution)/shard_map/all_to_all | solution.py:50
  277.9 6.8 %copy-start.3 = (f32[16,128]{1,0:T(8,128)}, f32[16,128]{1,0:T(8,128)S(1)}, u32[]{:S(2)}) copy-start(f32[16,128]{1,0:T(8,128)S(1)} %fusion.8) | copy-start | bytes 24580
